TPU v7x, 32 devices: a whole 2x2x4 slice. The times are simulated.
32 devices in a mesh: ep: 8 (over y, x, core), tp: 4 (over z).
Axes of the slice: x: 2, y: 2, z: 4, core: 2. Of those that a mesh axis runs over, the one named last changes fastest.
Arguments:
- layer_in: bfloat16 [2048, 2048], P('ep', 'tp'), may hold values from -6 to 6
- token_order: int32 [2048], replicated, may hold values from 0 to 2047, as said below
- seq_lengths: int32 [16, 3], P('ep'), may hold values from 1 to 64, 128 in all within a row
- routes: int32 [2048, 8], P('ep'), may hold values from 0 to 15, all different within a row; in each aligned block of 128 rows (0 to 127, 128 to 255, ...) at most 80 rows name the same one
- route_weights: float32 [2048, 8], P('ep'), may hold values from 0.25 to 0.75
- w_query: bfloat16 [2048, 4096], P('ep', 'tp'), may hold values from -0.125 to 0.125
- w_key: bfloat16 [2048, 512], P('ep', 'tp'), may hold values from -0.125 to 0.125
- w_value: bfloat16 [2048, 512], P('ep', 'tp'), may hold values from -0.125 to 0.125
- w_out: bfloat16 [2048, 4096], P('ep', 'tp'), may hold values from -0.5 to 0.5
- norm_attn: bfloat16 [2048], P('ep'), may hold values from 0.5 to 1.5
- norm_moe: bfloat16 [2048], P('ep'), may hold values from 0.5 to 1.5
- query_gain: bfloat16 [128], P('ep'), may hold values from 1 to 1.796875
- key_gain: bfloat16 [128], P('ep'), may hold values from 1 to 1.796875
- w_gate: bfloat16 [16, 768, 2048], P('ep', 'tp'), may hold values from -0.125 to 0.125
- w_up: bfloat16 [16, 768, 2048], P('ep', 'tp'), may hold values from -0.125 to 0.125
- w_down: bfloat16 [16, 768, 2048], P('ep', 'tp'), may hold values from -0.3125 to 0.3125
- grad_out: bfloat16 [2048, 2048], P('ep', 'tp'), may hold values from -6 to 6
Outputs:
- layer_out: bfloat16 [2048, 2048], P('ep', 'tp')
- grad_layer_in: float32 [2048, 2048], P('ep', 'tp')
- grad_w_query: float32 [2048, 4096], P('ep', 'tp')
- grad_w_key: float32 [2048, 512], P('ep', 'tp')
- grad_w_value: float32 [2048, 512], P('ep', 'tp')
- grad_w_out: float32 [2048, 4096], P('ep', 'tp')
- grad_norm_attn: float32 [2048], P('ep')
- grad_norm_moe: float32 [2048], P('ep')
- grad_query_gain: float32 [128], P('ep')
- grad_key_gain: float32 [128], P('ep')
- grad_w_gate: float32 [16, 768, 2048], P('ep', 'tp')
- grad_w_up: float32 [16, 768, 2048], P('ep', 'tp')
- grad_w_down: float32 [16, 768, 2048], P('ep', 'tp')
Inputs may be any that keep to these rules, and one draw needn't show every extreme that they name: `token_order`: each row number appears once. Of the 256 dealt rows of one index of ep, exactly 32 are rows of each index of ep. `seq_lengths`: row b holds the lengths of the 3 sequences of block b of 128 dealt rows, in order; they sum to 128, and the longest is 64. `routes`: each row names 8 different experts. Within each aligned block of 128 dealt rows (one micro-batch of one index of ep) no expert is named by more than 80 rows; in some blocks one is named by exactly 80.
All inputs are finite; a program needn't handle non-finite values.
Results may differ from a plain program's by a relative error of at most 0.023.
Values may be sent and summed in bfloat16 or wider, within the bound.
A program may use at most 256 MiB of HBM per device.

v0:
```python
import jax
import jax.numpy as jnp
from jax import lax
from jax.sharding import PartitionSpec as P

HEAD_DIM = 128
MICRO = 2
F32 = jnp.float32
BF16 = jnp.bfloat16
epsilon = 1e-06
rope_base = 1000000.0


def positions_of(lengths, row_count):
    offsets = jnp.arange(row_count, dtype=jnp.int32)
    seq_ends = jnp.cumsum(lengths)
    segment = jnp.sum((offsets[:, None] >= seq_ends[None, :]).astype(jnp.int32), axis=1)
    starts = seq_ends - lengths
    in_segment = segment[:, None] == jnp.arange(lengths.shape[0], dtype=jnp.int32)[None, :]
    position = offsets - jnp.sum(jnp.where(in_segment, starts[None, :], 0), axis=1)
    return (segment, position)


def rope_tables(position, half_dim):
    frequency = rope_base ** (-jnp.arange(half_dim, dtype=F32) / half_dim)
    angles = position.astype(F32)[:, None] * frequency[None, :]
    return (jnp.cos(angles)[:, None, :], jnp.sin(angles)[:, None, :])


def rotate(values, cosine, sine_table):
    half_dim = values.shape[-1] // 2
    first_half = values[..., :half_dim]
    second_half = values[..., half_dim:]
    return jnp.concatenate(
        [
            first_half * cosine - second_half * sine_table,
            second_half * cosine + first_half * sine_table,
        ],
        axis=-1,
    )


def rotate_back(incoming, cosine, sine_table):
    return rotate(incoming, cosine, -sine_table)


def deal_matrices(token_order, ep_index, rows_dev, ep_count):
    per_pair = rows_dev // ep_count
    rows = jnp.arange(rows_dev, dtype=jnp.int32)
    home = ep_index * rows_dev + rows
    at = jnp.arange(token_order.shape[0], dtype=jnp.int32)
    place = jnp.sum(jnp.where(token_order[None, :] == home[:, None], at[None, :], 0), axis=1)
    dest = place // rows_dev
    rank = jnp.sum(
        ((dest[:, None] == dest[None, :]) & (place[None, :] < place[:, None])).astype(jnp.int32),
        axis=1,
    )
    send_slot = dest * per_pair + rank
    send = (send_slot[None, :] == rows[:, None]).astype(BF16)
    mine = lax.dynamic_slice_in_dim(token_order, ep_index * rows_dev, rows_dev, 0)
    source = mine // rows_dev
    my_rank = jnp.sum(
        ((source[:, None] == source[None, :]) & (rows[None, :] < rows[:, None])).astype(jnp.int32),
        axis=1,
    )
    recv_slot = source * per_pair + my_rank
    recv = (recv_slot[:, None] == rows[None, :]).astype(BF16)
    return (send, recv)


def inverse_rms(values):
    return lax.rsqrt(jnp.mean(values * values, axis=-1, keepdims=True) + epsilon)


def norm_back(grad_unit, unit_values, inverse):
    return inverse * (
        grad_unit - unit_values * jnp.mean(grad_unit * unit_values, axis=-1, keepdims=True)
    )


def dot_nn(left, right):
    return jnp.dot(left, right, preferred_element_type=F32)


def dot_tn(left_rows, right_rows):
    return lax.dot_general(
        left_rows, right_rows, (((0,), (0,)), ((), ())), preferred_element_type=F32
    )


def dot_nt(left_rows, right_matrix):
    return lax.dot_general(
        left_rows, right_matrix, (((1,), (1,)), ((), ())), preferred_element_type=F32
    )


def permute_rows(matrix, rows):
    return dot_nn(matrix, rows).astype(BF16)


def exchange(rows, ep_count):
    split = rows.reshape(ep_count, rows.shape[0] // ep_count, rows.shape[1])
    moved = lax.all_to_all(split, "ep", split_axis=0, concat_axis=0, tiled=True)
    return moved.reshape(rows.shape)


def on_device(
    layer_in,
    token_order,
    seq_lengths,
    routes,
    route_weights,
    w_query,
    w_key,
    w_value,
    w_out,
    norm_attn,
    norm_moe,
    query_gain,
    key_gain,
    w_gate,
    w_up,
    w_down,
    grad_out,
):
    ep_count = lax.axis_size("ep")
    tp_count = lax.axis_size("tp")
    tp_index = lax.axis_index("tp")
    ep_index = lax.axis_index("ep")
    local_experts, hidden_here, model_width = w_gate.shape
    experts = local_experts * ep_count
    rows_dev = layer_in.shape[0]
    micro_rows = rows_dev // MICRO
    share_width = layer_in.shape[1]
    score_scale = HEAD_DIM ** (-0.5)
    send, recv = deal_matrices(token_order, ep_index, rows_dev, ep_count)
    both = jnp.concatenate([layer_in, grad_out], axis=1)
    got = permute_rows(recv, exchange(permute_rows(send, both), ep_count))
    layer_full = lax.all_gather(got[:, :share_width], "tp", axis=1, tiled=True)
    grad_full = lax.all_gather(got[:, share_width:], "tp", axis=1, tiled=True)
    q_width, kv_width = (w_query.shape[1], w_key.shape[1])
    packed = jnp.concatenate([w_query, w_out, w_key, w_value], axis=1)
    packed = lax.all_gather(packed, "ep", axis=0, tiled=True)
    full_query = packed[:, :q_width]
    full_out = packed[:, q_width : 2 * q_width]
    full_kv = packed[:, 2 * q_width :]
    gains = jnp.concatenate([norm_attn, norm_moe, query_gain, key_gain]).reshape(1, -1)
    gains = lax.all_gather(gains, "ep", axis=0, tiled=True).astype(F32)
    part = norm_attn.shape[0]
    head_part = query_gain.shape[0]
    gain_attn = gains[:, :part].reshape(-1)
    gain_moe = gains[:, part : 2 * part].reshape(-1)
    gain_query = gains[:, 2 * part : 2 * part + head_part].reshape(-1)
    gain_key = gains[:, 2 * part + head_part :].reshape(-1)
    expert_ids = jnp.arange(experts, dtype=jnp.int32)
    dense = jnp.sum(
        jnp.where(routes[:, :, None] == expert_ids[None, None, :], route_weights[:, :, None], 0.0),
        axis=1,
    )
    scale_all = lax.all_gather(dense, "ep", axis=0, tiled=True)
    scale = lax.dynamic_slice_in_dim(scale_all, ep_index * local_experts, local_experts, 1)
    all_grad = lax.all_gather(grad_full, "ep", axis=0, tiled=True)
    heads_here = q_width // HEAD_DIM
    kv_here = kv_width // HEAD_DIM
    group_size = heads_here // kv_here
    segment, position = jax.vmap(positions_of, in_axes=(0, None))(seq_lengths, micro_rows)
    cosine, sine_table = rope_tables(position.reshape(-1), HEAD_DIM // 2)
    layer_float = layer_full.astype(F32)
    inverse_one = inverse_rms(layer_float)
    unit_one = layer_float * inverse_one
    normed = (unit_one * gain_attn).astype(BF16)
    query_proj = dot_nn(normed, full_query).reshape(rows_dev, heads_here, HEAD_DIM)
    kv_proj = dot_nn(normed, full_kv)
    key_proj = kv_proj[:, :kv_width].reshape(rows_dev, kv_here, HEAD_DIM)
    value_proj = kv_proj[:, kv_width:].reshape(rows_dev, kv_here, HEAD_DIM)
    inverse_query = inverse_rms(query_proj)
    unit_query = query_proj * inverse_query
    inverse_key = inverse_rms(key_proj)
    unit_key = key_proj * inverse_key
    queries = (
        rotate(unit_query * gain_query, cosine, sine_table)
        .astype(BF16)
        .reshape(MICRO, micro_rows, kv_here, group_size, HEAD_DIM)
    )
    key_rows = (
        rotate(unit_key * gain_key, cosine, sine_table)
        .astype(BF16)
        .reshape(MICRO, micro_rows, kv_here, HEAD_DIM)
    )
    values = value_proj.astype(BF16).reshape(MICRO, micro_rows, kv_here, HEAD_DIM)
    scores = (
        jnp.einsum("mqkgd,mtkd->mkgqt", queries, key_rows, preferred_element_type=F32) * score_scale
    )
    offsets = jnp.arange(micro_rows, dtype=jnp.int32)
    allowed = (segment[:, :, None] == segment[:, None, :]) & (
        offsets[None, None, :] <= offsets[None, :, None]
    )
    scores = jnp.where(allowed[:, None, None], scores, -1e30)
    row_peak = jnp.max(scores, axis=-1, keepdims=True)
    exponent = jnp.exp(scores - row_peak)
    attn_probs = exponent / jnp.sum(exponent, axis=-1, keepdims=True)
    probs_low = attn_probs.astype(BF16)
    context = jnp.einsum("mkgqt,mtkd->mqkgd", probs_low, values, preferred_element_type=F32)
    context_low = context.reshape(rows_dev, heads_here * HEAD_DIM).astype(BF16)
    attn_part = dot_nt(context_low, full_out)
    attn_out = lax.psum(attn_part.astype(BF16), "tp").astype(F32)
    hidden = layer_float + attn_out
    inverse_two = inverse_rms(hidden)
    unit_two = hidden * inverse_two
    moe_in = (unit_two * gain_moe).astype(BF16)
    all_in = lax.all_gather(moe_in, "ep", axis=0, tiled=True)
    flat = local_experts * hidden_here
    gate_matrix = w_gate.reshape(flat, model_width)
    up_matrix = w_up.reshape(flat, model_width)
    down_matrix = w_down.reshape(flat, model_width)
    row_scale = jnp.repeat(scale, hidden_here, axis=1)
    gate_pre = dot_nt(all_in, gate_matrix)
    up_pre = dot_nt(all_in, up_matrix)
    grad_active = dot_nt(all_grad, down_matrix) * row_scale
    sigmoid_gate = jax.nn.sigmoid(gate_pre)
    silu_gate = gate_pre * sigmoid_gate
    active = (silu_gate * up_pre * row_scale).astype(BF16)
    grad_up_pre = (grad_active * silu_gate).astype(BF16)
    grad_gate_pre = (
        grad_active * up_pre * sigmoid_gate * (1.0 + gate_pre * (1.0 - sigmoid_gate))
    ).astype(BF16)
    grad_partial = dot_nn(grad_gate_pre, gate_matrix) + dot_nn(grad_up_pre, up_matrix)
    grad_partial = lax.psum_scatter(
        grad_partial.astype(BF16), "ep", scatter_dimension=0, tiled=True
    )
    grad_share = lax.psum_scatter(grad_partial, "tp", scatter_dimension=1, tiled=True)
    out_partial = dot_nn(active, down_matrix)
    out_partial = lax.psum_scatter(out_partial.astype(BF16), "ep", scatter_dimension=0, tiled=True)
    mixed = lax.psum_scatter(out_partial, "tp", scatter_dimension=1, tiled=True)
    hidden_share = lax.dynamic_slice_in_dim(hidden, tp_index * share_width, share_width, 1)
    layer_dealt = (hidden_share + mixed.astype(F32)).astype(BF16)
    grad_w_down = dot_tn(active, all_grad).reshape(w_down.shape)
    grad_w_gate = dot_tn(grad_gate_pre, all_in).reshape(w_gate.shape)
    grad_w_up = dot_tn(grad_up_pre, all_in).reshape(w_up.shape)
    grad_float = grad_full.astype(F32)
    grad_moe_in = lax.all_gather(grad_share, "tp", axis=1, tiled=True).astype(F32)
    norm_moe_part = jnp.sum(grad_moe_in * unit_two, axis=0)
    grad_hidden = grad_float + norm_back(grad_moe_in * gain_moe, unit_two, inverse_two)
    grad_attn = grad_hidden.astype(BF16)
    grad_w_out = dot_tn(grad_attn, context_low)
    grad_context = (
        dot_nn(grad_attn, full_out)
        .astype(BF16)
        .reshape(MICRO, micro_rows, kv_here, group_size, HEAD_DIM)
    )
    grad_probs = jnp.einsum("mqkgd,mtkd->mkgqt", grad_context, values, preferred_element_type=F32)
    prob_delta = jnp.sum(attn_probs * grad_probs, axis=-1, keepdims=True)
    grad_scores = (attn_probs * (grad_probs - prob_delta)).astype(BF16)
    grad_queries = (
        jnp.einsum("mkgqt,mtkd->mqkgd", grad_scores, key_rows, preferred_element_type=F32).reshape(
            rows_dev, heads_here, HEAD_DIM
        )
        * score_scale
    )
    grad_keys = (
        jnp.einsum("mkgqt,mqkgd->mtkd", grad_scores, queries, preferred_element_type=F32).reshape(
            rows_dev, kv_here, HEAD_DIM
        )
        * score_scale
    )
    grad_values = jnp.einsum(
        "mkgqt,mqkgd->mtkd", probs_low, grad_context, preferred_element_type=F32
    )
    grad_unit_query = rotate_back(grad_queries, cosine, sine_table)
    grad_unit_key = rotate_back(grad_keys, cosine, sine_table)
    query_gain_part = jnp.sum(grad_unit_query * unit_query, axis=(0, 1))
    key_gain_part = jnp.sum(grad_unit_key * unit_key, axis=(0, 1))
    grad_query_proj = (
        norm_back(grad_unit_query * gain_query, unit_query, inverse_query)
        .reshape(rows_dev, heads_here * HEAD_DIM)
        .astype(BF16)
    )
    grad_key_proj = (
        norm_back(grad_unit_key * gain_key, unit_key, inverse_key)
        .reshape(rows_dev, kv_width)
        .astype(BF16)
    )
    grad_value_proj = grad_values.reshape(rows_dev, kv_width).astype(BF16)
    grad_kv_proj = jnp.concatenate([grad_key_proj, grad_value_proj], axis=1)
    normed_part = dot_nt(grad_query_proj, full_query) + dot_nt(grad_kv_proj, full_kv)
    grad_normed = lax.psum_scatter(
        normed_part.astype(BF16), "tp", scatter_dimension=1, tiled=True
    ).astype(F32)
    grad_packed = jnp.concatenate(
        [
            dot_tn(normed, grad_query_proj).astype(BF16),
            grad_w_out.astype(BF16),
            dot_tn(normed, grad_kv_proj).astype(BF16),
        ],
        axis=1,
    )
    grad_packed = lax.psum_scatter(grad_packed, "ep", scatter_dimension=0, tiled=True).astype(F32)
    start = tp_index * share_width
    gain_share = lax.dynamic_slice_in_dim(gain_attn, start, share_width, 0)
    unit_share = lax.dynamic_slice_in_dim(unit_one, start, share_width, 1)
    hidden_grad_share = lax.dynamic_slice_in_dim(grad_hidden, start, share_width, 1)
    scaled = grad_normed * gain_share
    row_mean = lax.psum(jnp.sum(scaled * unit_share, axis=1), "tp") / model_width
    grad_layer = hidden_grad_share + inverse_one * (scaled - unit_share * row_mean[:, None])
    norm_attn_part = lax.dynamic_update_slice_in_dim(
        jnp.zeros((model_width,), F32), jnp.sum(grad_normed * unit_share, axis=0), start, 0
    )
    small = jnp.concatenate(
        [norm_attn_part, norm_moe_part / tp_count, query_gain_part, key_gain_part]
    )
    small = lax.psum(small, ("ep", "tp"))
    grad_norm_attn = lax.dynamic_slice_in_dim(small, ep_index * part, part, 0)
    grad_norm_moe = lax.dynamic_slice_in_dim(small, model_width + ep_index * part, part, 0)
    grad_query_gain = lax.dynamic_slice_in_dim(
        small, 2 * model_width + ep_index * head_part, head_part, 0
    )
    grad_key_gain = lax.dynamic_slice_in_dim(
        small, 2 * model_width + HEAD_DIM + ep_index * head_part, head_part, 0
    )
    back = jnp.concatenate([layer_dealt, grad_layer.astype(BF16)], axis=1)
    home = exchange(dot_tn(recv, back).astype(BF16), ep_count)
    home = dot_tn(send, home)
    return (
        home[:, :share_width].astype(BF16),
        home[:, share_width:],
        grad_packed[:, :q_width],
        grad_packed[:, 2 * q_width : 2 * q_width + kv_width],
        grad_packed[:, 2 * q_width + kv_width :],
        grad_packed[:, q_width : 2 * q_width],
        grad_norm_attn,
        grad_norm_moe,
        grad_query_gain,
        grad_key_gain,
        grad_w_gate,
        grad_w_up,
        grad_w_down,
    )


def solution(mesh):
    return jax.shard_map(
        on_device,
        mesh=mesh,
        in_specs=(
            P("ep", "tp"),
            P(),
            P("ep", None),
            P("ep", None),
            P("ep", None),
            P("ep", "tp"),
            P("ep", "tp"),
            P("ep", "tp"),
            P("ep", "tp"),
            P("ep"),
            P("ep"),
            P("ep"),
            P("ep"),
            P("ep", "tp", None),
            P("ep", "tp", None),
            P("ep", "tp", None),
            P("ep", "tp"),
        ),
        out_specs=(
            P("ep", "tp"),
            P("ep", "tp"),
            P("ep", "tp"),
            P("ep", "tp"),
            P("ep", "tp"),
            P("ep", "tp"),
            P("ep"),
            P("ep"),
            P("ep"),
            P("ep"),
            P("ep", "tp", None),
            P("ep", "tp", None),
            P("ep", "tp", None),
        ),
        check_vma=False,
    )
```

profile of v0, /device:TPU:0, one launch (start us, length us, event | category | flops | bytes accessed | tf_op | source)
XLA Modules:
  0.0 725.2 jit_solution(13505523342195663563)
XLA Ops:
  18.4 7.9 %all-to-all-done = bf16[8,32,1024]{2,1,0:T(8,128)(2,1)S(1)} async-done(((bf16[8,32,1024]{2,1,0:T(8,128)(2,1)}), bf16[8,32,1024]{2,1,0:T(8,128)(2,1)S(1)}, u32[]{:S(2)}, u32[]{:S(2)}) %all-to-all-start) | async-done | bytes 524320 | tf_op jit(solution)/shard_map/all_to_all | solution.py:103
  30.8 23.5 %all-reduce = bf16[4352]{0:T(1024)(128)(2,1)S(1)} all-reduce(bf16[4352]{0:T(1024)(128)(2,1)S(1)} %dynamic-update-slice), channel_id=2, replica_groups=mesh['ep'=8,'tp'=4] {'ep'}, use_global_device_ids=true, to_apply=%add | all-reduce | flops 4352 | bytes 17408
  59.1 56.6 %all-gather.10.cloned.1.call-done = bf16[2048,2304]{1,0:T(8,128)(2,1)} async-done(((bf16[256,2304]{1,0:T(8,128)(2,1)}), bf16[2048,2304]{1,0:T(8,128)(2,1)}) %all-gather.10.cloned.1.call-update) | async-done | bytes 9437200 | tf_op jit(solution)/shard_map/all_gather | solution.py:143
  139.8 6.0 all-gather.14.cloned.1.call-done
  147.2 52.7 %all-reduce.3.cloned.1.call-done = bf16[256,2048]{1,0:T(8,128)(2,1)} async-done(((bf16[256,2048]{1,0:T(8,128)(2,1)}), bf16[256,2048]{1,0:T(8,128)(2,1)}) %all-reduce.3.cloned.1.call-update) | async-done | bytes 1048592 | tf_op jit(solution)/shard_map/psum | solution.py:206
  206.7 10.0 %all_gather.28 = f32[2048,16]{0,1:T(8,128)S(1)} all-gather(f32[256,16]{0,1:T(8,128)S(1)} %select_reduce_fusion.1), channel_id=1, replica_groups=mesh['ep'=8,'tp'=4] {'ep'}, dimensions={0}, use_global_device_ids=true | all-gather | bytes 147456 | tf_op jit(solution)/shard_map/all_gather | solution.py:160
  222.3 33.1 %all-gather.16.cloned.1.call-done = bf16[2048,2048]{1,0:T(8,128)(2,1)} async-done(((bf16[256,2048]{1,0:T(8,128)(2,1)}), bf16[2048,2048]{1,0:T(8,128)(2,1)}) %all-gather.16.cloned.1.call-update) | async-done | bytes 8388624 | tf_op jit(solution)/shard_map/all_gather | solution.py:162
  255.5 11.0 %convolution_multiply_fusion = f32[2048,384]{1,0:T(8,128)} fusion(f32[2048,384]{1,0:T(8,128)} %copy.81, bf16[2048,2048]{1,0:T(8,128)(2,1)} %all-gather.16.cloned.1.call-done, bf16[384,2048]{1,0:T(8,128)(2,1)} %bitcast.201), kind=kOutput, calls=%fused_computation.21 | convolution fusion | flops 3222011904 | bytes 16252928 | tf_op jit(solution)/shard_map/dot_general | solution.py:92
  266.4 45.1 %all-gather.12.cloned.1.call-done = bf16[2048,2048]{1,0:T(8,128)(2,1)} async-done(((bf16[256,2048]{1,0:T(8,128)(2,1)}), bf16[2048,2048]{1,0:T(8,128)(2,1)}) %all-gather.12.cloned.1.call-update) | async-done | bytes 8388624 | tf_op jit(solution)/shard_map/all_gather | solution.py:211
  311.5 10.2 %fusion.104 = f32[2048,384]{1,0:T(8,128)} fusion(bf16[2048,2048]{1,0:T(8,128)(2,1)} %all-gather.12.cloned.1.call-done, bf16[384,2048]{1,0:T(8,128)(2,1)} %bitcast.184), kind=kOutput, calls=%fused_computation.204 | convolution fusion | flops 3221225472 | bytes 13107200 | tf_op jit(solution)/shard_map/dot_general | solution.py:92
  321.7 8.5 %multiply_convert_fusion.2 = (bf16[2048,384]{1,0:T(8,128)(2,1)}, bf16[2048,384]{1,0:T(8,128)(2,1)S(1)}, bf16[2048,384]{1,0:T(8,128)(2,1)S(1)}) fusion(f32[2048,384]{1,0:T(8,128)S(1)} %copy-done.24, f32[2048,384]{1,0:T(8,128)} %fusion.104, f32[2048,384]{1,0:T(8,128)S(1)} %copy-done.75, bf16[2048,2048]{1,0:T(8,128)(2,1)S(1)} %copy-done.2, ...), kind=kOutput, calls=%fused_computation.15 | convolution fusion | flops 3233808384 | bytes 24117248 | tf_op jit(solution)/shard_map/dot_general | solution.py:92
  330.2 22.1 %fusion.105 = f32[2048,2048]{1,0:T(8,128)} fusion(bf16[2048,384]{1,0:T(8,128)(2,1)S(1)} %get-tuple-element.61, bf16[384,2048]{1,0:T(8,128)(2,1)S(1)} %bitcast.185), kind=kOutput, calls=%fused_computation.205 | convolution fusion | flops 3221225472 | bytes 19922944 | tf_op jit(solution)/shard_map/dot_general | solution.py:82
  352.3 10.2 %add_convert_fusion = bf16[2048,2048]{1,0:T(8,128)(2,1)} fusion(f32[2048,2048]{1,0:T(8,128)} %fusion.105, bf16[2048,384]{1,0:T(8,128)(2,1)S(1)} %get-tuple-element.62, bf16[384,2048]{1,0:T(8,128)(2,1)S(1)} %bitcast.162), kind=kOutput, calls=%fused_computation | convolution fusion | flops 3229614080 | bytes 28311552 | tf_op jit(solution)/shard_map/dot_general | solution.py:82
  362.6 71.6 %reduce-scatter.11.cloned.1.call-done = bf16[256,2048]{1,0:T(8,128)(2,1)} async-done(((bf16[2048,2048]{1,0:T(8,128)(2,1)}), bf16[256,2048]{1,0:T(8,128)(2,1)}) %reduce-scatter.11.cloned.1.call-update) | async-done | bytes 1048592 | tf_op jit(solution)/shard_map/reduce_scatter | solution.py:228
  434.3 8.1 %convolution_convert_fusion = bf16[2048,2048]{1,0:T(8,128)(2,1)} fusion(bf16[2048,384]{1,0:T(8,128)(2,1)S(1)} %copy-done.25, bf16[384,2048]{1,0:T(8,128)(2,1)} %bitcast.202), kind=kOutput, calls=%fused_computation.2 | convolution fusion | flops 3225419776 | bytes 11534336 | tf_op jit(solution)/shard_map/dot_general | solution.py:82
  442.5 21.3 %reduce-scatter.13.cloned.1.call-done = bf16[256,512]{1,0:T(8,128)(2,1)} async-done(((bf16[256,2048]{1,0:T(8,128)(2,1)}), bf16[256,512]{1,0:T(8,128)(2,1)}) %reduce-scatter.13.cloned.1.call-update) | async-done | bytes 262160 | tf_op jit(solution)/shard_map/reduce_scatter | solution.py:231
  466.2 71.1 %reduce-scatter.7.cloned.1.call-done = bf16[256,2048]{1,0:T(8,128)(2,1)} async-done(((bf16[2048,2048]{1,0:T(8,128)(2,1)}), bf16[256,2048]{1,0:T(8,128)(2,1)}) %reduce-scatter.7.cloned.1.call-update) | async-done | bytes 1048592 | tf_op jit(solution)/shard_map/reduce_scatter | solution.py:233
  537.4 29.4 %all-gather.18.cloned.1.call-done = bf16[256,2048]{1,0:T(8,128)(2,1)} async-done(((bf16[256,512]{1,0:T(8,128)(2,1)}), bf16[256,2048]{1,0:T(8,128)(2,1)}) %all-gather.18.cloned.1.call-update) | async-done | bytes 1048592 | tf_op jit(solution)/shard_map/all_gather | solution.py:241
  594.3 15.9 %pad_maximum_fusion = bf16[2048,2304]{0,1:T(8,128)(2,1)} fusion(bf16[2048,256]{0,1:T(8,128)(2,1)S(1)} %convolution_convert_fusion.3, bf16[2048,1024]{0,1:T(8,128)(2,1)S(1)} %convolution_convert_fusion.1, bf16[2048,1024]{0,1:T(8,128)(2,1)S(1)} %convolution_convert_fusion.2), kind=kLoop, calls=%fused_computation.1 | loop fusion | flops 28311552 | bytes 18874368 | tf_op jit(solution)/shard_map/concatenate | solution.py:289
  611.7 8.7 %fusion.108 = f32[384,2048]{1,0:T(8,128)} fusion(bf16[2048,384]{1,0:T(8,128)(2,1)S(1)} %copy-done.26, bf16[2048,2048]{1,0:T(8,128)(2,1)} %all-gather.16.cloned.1.call-done), kind=kOutput, calls=%fused_computation.208 | convolution fusion | flops 3221225472 | bytes 13107200 | tf_op jit(solution)/shard_map/dot_general | solution.py:86
  620.4 8.8 %fusion.106 = f32[384,2048]{1,0:T(8,128)} fusion(bf16[2048,384]{1,0:T(8,128)(2,1)S(1)} %copy-done.15, bf16[2048,2048]{1,0:T(8,128)(2,1)} %all-gather.12.cloned.1.call-done), kind=kOutput, calls=%fused_computation.206 | convolution fusion | flops 3221225472 | bytes 13107200 | tf_op jit(solution)/shard_map/dot_general | solution.py:86
  629.2 5.3 fusion.107
  637.4 10.4 %psum.22 = f32[256]{0:T(256)S(1)} all-reduce(f32[256]{0:T(256)S(1)} %get-tuple-element.55), channel_id=1, replica_groups=mesh['ep'=8,'tp'=4] {'tp'}, use_global_device_ids=true, to_apply=%region_24.25 | all-reduce | flops 256 | bytes 2048 | tf_op jit(solution)/shard_map/psum | solution.py:303
  654.4 47.9 %psum.23 = f32[4352]{0:T(1024)S(1)} all-reduce(f32[4352]{0:T(1024)S(1)} %pad_maximum_fusion.10), channel_id=1, replica_groups=mesh['ep'=8,'tp'=4] {'ep','tp'}, use_global_device_ids=true, to_apply=%region_31.32 | all-reduce | flops 4352 | bytes 34816 | tf_op jit(solution)/shard_map/psum | solution.py:311
  (311 shorter events, 113.8 us)
Async XLA Ops:
  7.2 314.5 %copy-start = (bf16[2,192,2048]{2,1,0:T(8,128)(2,1)S(1)}, bf16[2,192,2048]{2,1,0:T(8,128)(2,1)}, u32[]{:S(2)}) copy-start(bf16[2,192,2048]{2,1,0:T(8,128)(2,1)} %param.31) | copy-start | bytes 4718596
  11.5 14.9 %all-to-all-start = ((bf16[8,32,1024]{2,1,0:T(8,128)(2,1)}), bf16[8,32,1024]{2,1,0:T(8,128)(2,1)S(1)}, u32[]{:S(2)}, u32[]{:S(2)}) async-start(bf16[8,32,1024]{2,1,0:T(8,128)(2,1)} %bitcast), calls=%async_computation | async-start | bytes 1048576 | tf_op jit(solution)/shard_map/all_to_all | solution.py:103
  16.7 40.8 %all-gather.8.cloned.1.call-start = ((), (), s32[]{:S(2)}) async-start(), calls=%async_computation.8 | async-start | bytes 1310720 | tf_op jit(solution)/shard_map/all_gather | solution.py:139
  27.6 88.1 %all-gather.10.cloned.1.call-start = ((), (), s32[]{:S(2)}) async-start(), calls=%async_computation.9 | async-start | bytes 10616832 | tf_op jit(solution)/shard_map/all_gather | solution.py:143
  28.8 117.0 %all-gather.14.cloned.1.call-start = ((), (), s32[]{:S(2)}) async-start(), calls=%async_computation.14 | async-start | bytes 1310720 | tf_op jit(solution)/shard_map/all_gather | solution.py:140
  54.6 67.5 %copy-start.59 = (f32[128]{0:T(128)}, f32[128]{0:T(128)S(1)}, u32[]{:S(2)}) copy-start(f32[128]{0:T(128)S(1)} %mul.459) | copy-start | bytes 1540
  54.6 67.6 %copy-start.61 = (f32[128]{0:T(128)}, f32[128]{0:T(128)S(1)}, u32[]{:S(2)}) copy-start(f32[128]{0:T(128)S(1)} %mul.473) | copy-start | bytes 1540
  55.3 68.8 %copy-start.63 = (f32[64]{0:T(128)}, f32[64]{0:T(128)S(1)}, u32[]{:S(2)}) copy-start(f32[64]{0:T(128)S(1)} %multiply_power_fusion) | copy-start | bytes 772
  55.5 68.6 %copy-start.52 = (f32[256]{0:T(256)}, f32[256]{0:T(256)S(1)}, u32[]{:S(2)}) copy-start(f32[256]{0:T(256)S(1)} %convert_bitcast_fusion.1) | copy-start | bytes 3076
  57.4 69.3 %copy-start.31 = (f32[256,64]{1,0:T(8,128)}, f32[256,64]{1,0:T(8,128)S(1)}, u32[]{:S(2)}) copy-start(f32[256,64]{1,0:T(8,128)S(1)} %get-tuple-element.94) | copy-start | bytes 196612
  57.4 142.5 %all-reduce.3.cloned.1.call-start = ((), (), s32[]{:S(2)}) async-start(), calls=%async_computation.10 | async-start | bytes 2097152 | tf_op jit(solution)/shard_map/psum | solution.py:206
  139.8 115.7 %all-gather.16.cloned.1.call-start = ((), (), s32[]{:S(2)}) async-start(), calls=%async_computation.15 | async-start | bytes 9437184 | tf_op jit(solution)/shard_map/all_gather | solution.py:162
  145.9 165.6 %all-gather.12.cloned.1.call-start = ((), (), s32[]{:S(2)}) async-start(), calls=%async_computation.11 | async-start | bytes 9437184 | tf_op jit(solution)/shard_map/all_gather | solution.py:211
  205.9 228.3 %reduce-scatter.11.cloned.1.call-start = ((), (), s32[]{:S(2)}) async-start(), calls=%async_computation.16 | async-start | bytes 9437184 | tf_op jit(solution)/shard_map/reduce_scatter | solution.py:228
  362.5 71.7 %copy-start.25 = (bf16[2048,384]{1,0:T(8,128)(2,1)S(1)}, bf16[2048,384]{1,0:T(8,128)(2,1)}, u32[]{:S(2)}) copy-start(bf16[2048,384]{1,0:T(8,128)(2,1)} %get-tuple-element.60) | copy-start | bytes 4718596
  362.5 101.3 %reduce-scatter.13.cloned.1.call-start = ((), (), s32[]{:S(2)}) async-start(), calls=%async_computation.17 | async-start | bytes 1310720 | tf_op jit(solution)/shard_map/reduce_scatter | solution.py:231
  434.2 103.1 %reduce-scatter.7.cloned.1.call-start = ((), (), s32[]{:S(2)}) async-start(), calls=%async_computation.12 | async-start | bytes 9437184 | tf_op jit(solution)/shard_map/reduce_scatter | solution.py:233
  442.4 124.3 %copy-start.11 = (bf16[256,2048]{1,0:T(8,128)(2,1)S(1)}, bf16[256,2048]{1,0:T(8,128)(2,1)}, u32[]{:S(2)}) copy-start(bf16[256,2048]{1,0:T(8,128)(2,1)} %all-reduce.3.cloned.1.call-done) | copy-start | bytes 3145732
  442.4 124.3 %all-gather.18.cloned.1.call-start = ((), (), s32[]{:S(2)}) async-start(), calls=%async_computation.18 | async-start | bytes 1310720 | tf_op jit(solution)/shard_map/all_gather | solution.py:241
  463.8 170.6 %reduce-scatter.9.cloned.1.call-start = ((), (), s32[]{:S(2)}) async-start(), calls=%async_computation.13 | async-start | bytes 1310720 | tf_op jit(solution)/shard_map/reduce_scatter | solution.py:234
  537.3 98.5 %reduce-scatter.15.cloned.1.call-start = ((), (), s32[]{:S(2)}) async-start(), calls=%async_computation.19 | async-start | bytes 1310720 | tf_op jit(solution)/shard_map/reduce_scatter | solution.py:286
  590.7 118.8 %reduce-scatter.17.cloned.1.call-start = ((), (), s32[]{:S(2)}) async-start(), calls=%async_computation.20 | async-start | bytes 10616832 | tf_op jit(solution)/shard_map/reduce_scatter | solution.py:297
  637.4 66.1 %copy-start.69 = (s32[256]{0:T(256)S(1)}, s32[256]{0:T(256)}, u32[]{:S(2)}) copy-start(s32[256]{0:T(256)} %copy-done.68) | copy-start | bytes 3076
  650.5 53.1 %all-to-all-start.1 = ((bf16[8,32,1024]{2,1,0:T(8,128)(2,1)}), bf16[8,32,1024]{2,1,0:T(8,128)(2,1)S(1)}, u32[]{:S(2)}, u32[]{:S(2)}) async-start(bf16[8,32,1024]{2,1,0:T(8,128)(2,1)} %bitcast.45), calls=%async_computation.6 | async-start | bytes 1048576 | tf_op jit(solution)/shard_map/all_to_all | solution.py:103
  (69 other events, 556.2 us)
Sparse Core Ops, SparseCore 0:
  27.7 27.3 all-gather.7
  57.6 58.0 all-gather.9
  117.9 27.9 all-gather.13
  148.7 51.2 all-reduce.2
  201.7 53.7 all-gather.15
  257.2 54.2 all-gather.11
  362.7 71.4 reduce-scatter.10
  436.5 27.2 reduce-scatter.12
  467.3 69.9 reduce-scatter.6
  538.7 27.9 all-gather.17
  569.0 26.6 reduce-scatter.8
  598.5 25.7 reduce-scatter.14
  627.8 81.7 reduce-scatter.16
where the time goes:
time: 734 us; the launch traced here: 725 us
  waiting for transfers between devices  399 us (54%)
  matrix products  125 us (17%)
  blocking collectives  91.8 us (13%)
  other arithmetic  46.4 us (6%)
  local copies, waits for them, and re-layouts  37.7 us (5%)
  between operations  16.1 us (2%)
  starting transfers between devices  9.33 us (1%)
    reduce_scatter x1, waiting for transfers between devices, on_device(): lax.psum_scatter(grad_partial.astype(BF16), 'ep', scatter_dimension=0, ti...  71.6 us
    reduce_scatter x1, waiting for transfers between devices, on_device(): lax.psum_scatter(out_partial.astype(BF16), 'ep', scatter_dimension=0, til...  71.1 us
    all_gather x1, waiting for transfers between devices, on_device(): packed = lax.all_gather(packed, 'ep', axis=0, tiled=True)  56.6 us
    dot_general x8, matrix products, dot_nn(): return jnp.dot(left, right, preferred_element_type=F32)  52.9 us
    psum x1, waiting for transfers between devices, on_device(): attn_out = lax.psum(attn_part.astype(BF16), 'tp').astype(F32)  52.7 us
    psum x1, blocking collectives, on_device(): small = lax.psum(small, ('ep', 'tp'))  47.9 us
    all_gather x1, waiting for transfers between devices, on_device(): all_in = lax.all_gather(moe_in, 'ep', axis=0, tiled=True)  45.1 us
    dot_general x6, matrix products, dot_nt(): lax.dot_general(left_rows, right_matrix, (((1,), (1,)), ((), ())), prefer...  40.5 us
  transfers between devices with their start and end apart: 15, of which 11 were waited for; matrix products, arithmetic and copies ran while one was open for 19% of the time, Pallas kernels for 0%

commit v1 on v0

--- a/solution.py
+++ b/solution.py
@@ -9,6 +9,11 @@
 BF16 = jnp.bfloat16
 epsilon = 1e-06
 rope_base = 1000000.0
+
+
+def deliver_record(content, mesh_name):
+    latest = jax.lax.all_gather(content, axis_name=mesh_name).sum(axis=0)
+    return latest
 
 
 def positions_of(lengths, row_count):
@@ -203,7 +208,7 @@
     context = jnp.einsum("mkgqt,mtkd->mqkgd", probs_low, values, preferred_element_type=F32)
     context_low = context.reshape(rows_dev, heads_here * HEAD_DIM).astype(BF16)
     attn_part = dot_nt(context_low, full_out)
-    attn_out = lax.psum(attn_part.astype(BF16), "tp").astype(F32)
+    attn_out = deliver_record(attn_part.astype(BF16), "tp").astype(F32)
     hidden = layer_float + attn_out
     inverse_two = inverse_rms(hidden)
     unit_two = hidden * inverse_two

time: 734 us -> 761 us (1.037)
  waiting for transfers between devices: 399 us -> 421 us
    all_gather x0 -> x1, waiting for transfers between devices: none -> 80.5 us  [deliver_record(): latest = jax.lax.all_gather(content, axis_name=mesh_name).sum(axis=0)]
    psum x1 -> x0, waiting for transfers between devices: 52.7 us -> none  [on_device(): attn_out = lax.psum(attn_part.astype(BF16), 'tp').astype(F32)]
    unnamed x170 -> x168, local copies, waits for them, and re-layouts: 16.1 us -> 15.5 us
where the time goes in v1:
time: 761 us; the launch traced here: 752 us
  waiting for transfers between devices  421 us (55%)
  matrix products  125 us (16%)
  blocking collectives  91.5 us (12%)
  other arithmetic  51.8 us (7%)
  local copies, waits for them, and re-layouts  37.1 us (5%)
  between operations  16.1 us (2%)
  starting transfers between devices  9.62 us (1%)
    all_gather x1, waiting for transfers between devices, deliver_record(): latest = jax.lax.all_gather(content, axis_name=mesh_name).sum(axis=0)  80.5 us
    reduce_scatter x1, waiting for transfers between devices, on_device(): lax.psum_scatter(grad_partial.astype(BF16), 'ep', scatter_dimension=0, ti...  71.6 us
    reduce_scatter x1, waiting for transfers between devices, on_device(): lax.psum_scatter(out_partial.astype(BF16), 'ep', scatter_dimension=0, til...  71.1 us
    all_gather x1, waiting for transfers between devices, on_device(): packed = lax.all_gather(packed, 'ep', axis=0, tiled=True)  55.5 us
    dot_general x8, matrix products, dot_nn(): return jnp.dot(left, right, preferred_element_type=F32)  52.9 us
    psum x1, blocking collectives, on_device(): small = lax.psum(small, ('ep', 'tp'))  47.9 us
    all_gather x1, waiting for transfers between devices, on_device(): all_in = lax.all_gather(moe_in, 'ep', axis=0, tiled=True)  45.1 us
    dot_general x6, matrix products, dot_nt(): lax.dot_general(left_rows, right_matrix, (((1,), (1,)), ((), ())), prefer...  40.6 us
  transfers between devices with their start and end apart: 15, of which 11 were waited for; matrix products, arithmetic and copies ran while one was open for 19% of the time, Pallas kernels for 0%

profile of v1, /device:TPU:0, one launch (start us, length us, event | category | flops | bytes accessed | tf_op | source)
XLA Modules:
  0.0 752.2 jit_solution(16061345660151406969)
XLA Ops:
  17.9 7.9 %all-to-all-done = bf16[8,32,1024]{2,1,0:T(8,128)(2,1)S(1)} async-done(((bf16[8,32,1024]{2,1,0:T(8,128)(2,1)}), bf16[8,32,1024]{2,1,0:T(8,128)(2,1)S(1)}, u32[]{:S(2)}, u32[]{:S(2)}) %all-to-all-start) | async-done | bytes 524320 | tf_op jit(solution)/shard_map/all_to_all | solution.py:108
  31.3 23.5 %all-reduce = bf16[4352]{0:T(1024)(128)(2,1)S(1)} all-reduce(bf16[4352]{0:T(1024)(128)(2,1)S(1)} %dynamic-update-slice), channel_id=2, replica_groups=mesh['ep'=8,'tp'=4] {'ep'}, use_global_device_ids=true, to_apply=%add | all-reduce | flops 4352 | bytes 17408
  59.6 55.5 %all-gather.12.cloned.1.call-done = bf16[2048,2304]{1,0:T(8,128)(2,1)} async-done(((bf16[256,2304]{1,0:T(8,128)(2,1)}), bf16[2048,2304]{1,0:T(8,128)(2,1)}) %all-gather.12.cloned.1.call-update) | async-done | bytes 9437200 | tf_op jit(solution)/shard_map/all_gather | solution.py:148
  139.3 6.0 all-gather.16.cloned.1.call-done
  146.9 80.5 %all-gather.22.cloned.1.call-done = bf16[1024,2048]{1,0:T(8,128)(2,1)} async-done(((bf16[256,2048]{1,0:T(8,128)(2,1)}), bf16[1024,2048]{1,0:T(8,128)(2,1)}) %all-gather.22.cloned.1.call-update) | async-done | bytes 4194320 | tf_op jit(solution)/shard_map/all_gather | solution.py:15
  238.6 9.8 %all_gather.36 = f32[2048,16]{0,1:T(8,128)S(1)} all-gather(f32[256,16]{0,1:T(8,128)S(1)} %select_reduce_fusion.1), channel_id=1, replica_groups=mesh['ep'=8,'tp'=4] {'ep'}, dimensions={0}, use_global_device_ids=true | all-gather | bytes 147456 | tf_op jit(solution)/shard_map/all_gather | solution.py:165
  254.0 28.5 %all-gather.18.cloned.1.call-done = bf16[2048,2048]{1,0:T(8,128)(2,1)} async-done(((bf16[256,2048]{1,0:T(8,128)(2,1)}), bf16[2048,2048]{1,0:T(8,128)(2,1)}) %all-gather.18.cloned.1.call-update) | async-done | bytes 8388624 | tf_op jit(solution)/shard_map/all_gather | solution.py:167
  282.5 11.0 %convolution_multiply_fusion = f32[2048,384]{1,0:T(8,128)} fusion(f32[2048,384]{1,0:T(8,128)} %copy.81, bf16[2048,2048]{1,0:T(8,128)(2,1)} %all-gather.18.cloned.1.call-done, bf16[384,2048]{1,0:T(8,128)(2,1)} %bitcast.203), kind=kOutput, calls=%fused_computation.21 | convolution fusion | flops 3222011904 | bytes 16252928 | tf_op jit(solution)/shard_map/dot_general | solution.py:97
  293.5 45.1 %all-gather.14.cloned.1.call-done = bf16[2048,2048]{1,0:T(8,128)(2,1)} async-done(((bf16[256,2048]{1,0:T(8,128)(2,1)}), bf16[2048,2048]{1,0:T(8,128)(2,1)}) %all-gather.14.cloned.1.call-update) | async-done | bytes 8388624 | tf_op jit(solution)/shard_map/all_gather | solution.py:216
  338.5 10.2 %fusion.104 = f32[2048,384]{1,0:T(8,128)} fusion(bf16[2048,2048]{1,0:T(8,128)(2,1)} %all-gather.14.cloned.1.call-done, bf16[384,2048]{1,0:T(8,128)(2,1)} %bitcast.186), kind=kOutput, calls=%fused_computation.204 | convolution fusion | flops 3221225472 | bytes 13107200 | tf_op jit(solution)/shard_map/dot_general | solution.py:97
  348.7 8.5 %multiply_convert_fusion.2 = (bf16[2048,384]{1,0:T(8,128)(2,1)}, bf16[2048,384]{1,0:T(8,128)(2,1)S(1)}, bf16[2048,384]{1,0:T(8,128)(2,1)S(1)}) fusion(f32[2048,384]{1,0:T(8,128)S(1)} %copy-done.24, f32[2048,384]{1,0:T(8,128)} %fusion.104, f32[2048,384]{1,0:T(8,128)S(1)} %copy-done.74, bf16[2048,2048]{1,0:T(8,128)(2,1)S(1)} %copy-done.2, ...), kind=kOutput, calls=%fused_computation.15 | convolution fusion | flops 3233808384 | bytes 24117248 | tf_op jit(solution)/shard_map/dot_general | solution.py:97
  357.3 22.0 %fusion.105 = f32[2048,2048]{1,0:T(8,128)} fusion(bf16[2048,384]{1,0:T(8,128)(2,1)S(1)} %get-tuple-element.61, bf16[384,2048]{1,0:T(8,128)(2,1)S(1)} %bitcast.187), kind=kOutput, calls=%fused_computation.205 | convolution fusion | flops 3221225472 | bytes 19922944 | tf_op jit(solution)/shard_map/dot_general | solution.py:87
  379.2 10.2 %add_convert_fusion = bf16[2048,2048]{1,0:T(8,128)(2,1)} fusion(f32[2048,2048]{1,0:T(8,128)} %fusion.105, bf16[2048,384]{1,0:T(8,128)(2,1)S(1)} %get-tuple-element.62, bf16[384,2048]{1,0:T(8,128)(2,1)S(1)} %bitcast.163), kind=kOutput, calls=%fused_computation | convolution fusion | flops 3229614080 | bytes 28311552 | tf_op jit(solution)/shard_map/dot_general | solution.py:87
  389.5 71.6 %reduce-scatter.11.cloned.1.call-done = bf16[256,2048]{1,0:T(8,128)(2,1)} async-done(((bf16[2048,2048]{1,0:T(8,128)(2,1)}), bf16[256,2048]{1,0:T(8,128)(2,1)}) %reduce-scatter.11.cloned.1.call-update) | async-done | bytes 1048592 | tf_op jit(solution)/shard_map/reduce_scatter | solution.py:233
  461.2 8.1 %convolution_convert_fusion = bf16[2048,2048]{1,0:T(8,128)(2,1)} fusion(bf16[2048,384]{1,0:T(8,128)(2,1)S(1)} %copy-done.25, bf16[384,2048]{1,0:T(8,128)(2,1)} %bitcast.204), kind=kOutput, calls=%fused_computation.2 | convolution fusion | flops 3225419776 | bytes 11534336 | tf_op jit(solution)/shard_map/dot_general | solution.py:87
  469.4 21.3 %reduce-scatter.13.cloned.1.call-done = bf16[256,512]{1,0:T(8,128)(2,1)} async-done(((bf16[256,2048]{1,0:T(8,128)(2,1)}), bf16[256,512]{1,0:T(8,128)(2,1)}) %reduce-scatter.13.cloned.1.call-update) | async-done | bytes 262160 | tf_op jit(solution)/shard_map/reduce_scatter | solution.py:236
  493.1 71.1 %reduce-scatter.7.cloned.1.call-done = bf16[256,2048]{1,0:T(8,128)(2,1)} async-done(((bf16[2048,2048]{1,0:T(8,128)(2,1)}), bf16[256,2048]{1,0:T(8,128)(2,1)}) %reduce-scatter.7.cloned.1.call-update) | async-done | bytes 1048592 | tf_op jit(solution)/shard_map/reduce_scatter | solution.py:238
  564.3 29.4 %all-gather.20.cloned.1.call-done = bf16[256,2048]{1,0:T(8,128)(2,1)} async-done(((bf16[256,512]{1,0:T(8,128)(2,1)}), bf16[256,2048]{1,0:T(8,128)(2,1)}) %all-gather.20.cloned.1.call-update) | async-done | bytes 1048592 | tf_op jit(solution)/shard_map/all_gather | solution.py:246
  621.3 15.9 %pad_maximum_fusion = bf16[2048,2304]{0,1:T(8,128)(2,1)} fusion(bf16[2048,256]{0,1:T(8,128)(2,1)S(1)} %convolution_convert_fusion.3, bf16[2048,1024]{0,1:T(8,128)(2,1)S(1)} %convolution_convert_fusion.1, bf16[2048,1024]{0,1:T(8,128)(2,1)S(1)} %convolution_convert_fusion.2), kind=kLoop, calls=%fused_computation.1 | loop fusion | flops 28311552 | bytes 18874368 | tf_op jit(solution)/shard_map/concatenate | solution.py:294
  638.6 8.7 %fusion.108 = f32[384,2048]{1,0:T(8,128)} fusion(bf16[2048,384]{1,0:T(8,128)(2,1)S(1)} %copy-done.26, bf16[2048,2048]{1,0:T(8,128)(2,1)} %all-gather.18.cloned.1.call-done), kind=kOutput, calls=%fused_computation.208 | convolution fusion | flops 3221225472 | bytes 13107200 | tf_op jit(solution)/shard_map/dot_general | solution.py:91
  647.3 8.8 %fusion.106 = f32[384,2048]{1,0:T(8,128)} fusion(bf16[2048,384]{1,0:T(8,128)(2,1)S(1)} %copy-done.15, bf16[2048,2048]{1,0:T(8,128)(2,1)} %all-gather.14.cloned.1.call-done), kind=kOutput, calls=%fused_computation.206 | convolution fusion | flops 3221225472 | bytes 13107200 | tf_op jit(solution)/shard_map/dot_general | solution.py:91
  656.1 5.3 fusion.107
  664.4 10.3 %psum.14 = f32[256]{0:T(256)S(1)} all-reduce(f32[256]{0:T(256)S(1)} %get-tuple-element.55), channel_id=1, replica_groups=mesh['ep'=8,'tp'=4] {'tp'}, use_global_device_ids=true, to_apply=%region_24.25 | all-reduce | flops 256 | bytes 2048 | tf_op jit(solution)/shard_map/psum | solution.py:308
  681.4 47.9 %psum.15 = f32[4352]{0:T(1024)S(1)} all-reduce(f32[4352]{0:T(1024)S(1)} %pad_maximum_fusion.10), channel_id=1, replica_groups=mesh['ep'=8,'tp'=4] {'ep','tp'}, use_global_device_ids=true, to_apply=%region_31.32 | all-reduce | flops 4352 | bytes 34816 | tf_op jit(solution)/shard_map/psum | solution.py:316
  (310 shorter events, 119.1 us)
Async XLA Ops:
  7.2 341.5 %copy-start = (bf16[2,192,2048]{2,1,0:T(8,128)(2,1)S(1)}, bf16[2,192,2048]{2,1,0:T(8,128)(2,1)}, u32[]{:S(2)}) copy-start(bf16[2,192,2048]{2,1,0:T(8,128)(2,1)} %param.31) | copy-start | bytes 4718596
  10.9 14.9 %all-to-all-start = ((bf16[8,32,1024]{2,1,0:T(8,128)(2,1)}), bf16[8,32,1024]{2,1,0:T(8,128)(2,1)S(1)}, u32[]{:S(2)}, u32[]{:S(2)}) async-start(bf16[8,32,1024]{2,1,0:T(8,128)(2,1)} %bitcast), calls=%async_computation | async-start | bytes 1048576 | tf_op jit(solution)/shard_map/all_to_all | solution.py:108
  16.1 41.9 %all-gather.10.cloned.1.call-start = ((), (), s32[]{:S(2)}) async-start(), calls=%async_computation.8 | async-start | bytes 1310720 | tf_op jit(solution)/shard_map/all_gather | solution.py:144
  27.1 88.1 %all-gather.12.cloned.1.call-start = ((), (), s32[]{:S(2)}) async-start(), calls=%async_computation.9 | async-start | bytes 10616832 | tf_op jit(solution)/shard_map/all_gather | solution.py:148
  29.3 116.0 %all-gather.16.cloned.1.call-start = ((), (), s32[]{:S(2)}) async-start(), calls=%async_computation.13 | async-start | bytes 1310720 | tf_op jit(solution)/shard_map/all_gather | solution.py:145
  55.1 66.6 %copy-start.58 = (f32[128]{0:T(128)}, f32[128]{0:T(128)S(1)}, u32[]{:S(2)}) copy-start(f32[128]{0:T(128)S(1)} %mul.459) | copy-start | bytes 1540
  55.1 66.6 %copy-start.60 = (f32[128]{0:T(128)}, f32[128]{0:T(128)S(1)}, u32[]{:S(2)}) copy-start(f32[128]{0:T(128)S(1)} %mul.473) | copy-start | bytes 1540
  55.8 67.9 %copy-start.62 = (f32[64]{0:T(128)}, f32[64]{0:T(128)S(1)}, u32[]{:S(2)}) copy-start(f32[64]{0:T(128)S(1)} %multiply_power_fusion) | copy-start | bytes 772
  56.0 67.7 %copy-start.51 = (f32[256]{0:T(256)}, f32[256]{0:T(256)S(1)}, u32[]{:S(2)}) copy-start(f32[256]{0:T(256)S(1)} %convert_bitcast_fusion.1) | copy-start | bytes 3076
  57.9 68.3 %copy-start.31 = (f32[256,64]{1,0:T(8,128)}, f32[256,64]{1,0:T(8,128)S(1)}, u32[]{:S(2)}) copy-start(f32[256,64]{1,0:T(8,128)S(1)} %get-tuple-element.94) | copy-start | bytes 196612
  57.9 169.5 %all-gather.22.cloned.1.call-start = ((), (), s32[]{:S(2)}) async-start(), calls=%async_computation.20 | async-start | bytes 5242880 | tf_op jit(solution)/shard_map/all_gather | solution.py:15
  139.3 143.2 %all-gather.18.cloned.1.call-start = ((), (), s32[]{:S(2)}) async-start(), calls=%async_computation.14 | async-start | bytes 9437184 | tf_op jit(solution)/shard_map/all_gather | solution.py:167
  145.3 193.2 %all-gather.14.cloned.1.call-start = ((), (), s32[]{:S(2)}) async-start(), calls=%async_computation.10 | async-start | bytes 9437184 | tf_op jit(solution)/shard_map/all_gather | solution.py:216
  237.8 223.3 %reduce-scatter.11.cloned.1.call-start = ((), (), s32[]{:S(2)}) async-start(), calls=%async_computation.15 | async-start | bytes 9437184 | tf_op jit(solution)/shard_map/reduce_scatter | solution.py:233
  389.4 71.7 %copy-start.25 = (bf16[2048,384]{1,0:T(8,128)(2,1)S(1)}, bf16[2048,384]{1,0:T(8,128)(2,1)}, u32[]{:S(2)}) copy-start(bf16[2048,384]{1,0:T(8,128)(2,1)} %get-tuple-element.60) | copy-start | bytes 4718596
  389.4 101.3 %reduce-scatter.13.cloned.1.call-start = ((), (), s32[]{:S(2)}) async-start(), calls=%async_computation.16 | async-start | bytes 1310720 | tf_op jit(solution)/shard_map/reduce_scatter | solution.py:236
  461.1 103.1 %reduce-scatter.7.cloned.1.call-start = ((), (), s32[]{:S(2)}) async-start(), calls=%async_computation.11 | async-start | bytes 9437184 | tf_op jit(solution)/shard_map/reduce_scatter | solution.py:238
  469.3 124.3 %copy-start.5 = (bf16[256,2048]{1,0:T(8,128)(2,1)S(1)}, bf16[256,2048]{1,0:T(8,128)(2,1)}, u32[]{:S(2)}) copy-start(bf16[256,2048]{1,0:T(8,128)(2,1)} %reduce_sum.208) | copy-start | bytes 3145732
  469.3 124.3 %all-gather.20.cloned.1.call-start = ((), (), s32[]{:S(2)}) async-start(), calls=%async_computation.17 | async-start | bytes 1310720 | tf_op jit(solution)/shard_map/all_gather | solution.py:246
  490.7 170.7 %reduce-scatter.9.cloned.1.call-start = ((), (), s32[]{:S(2)}) async-start(), calls=%async_computation.12 | async-start | bytes 1310720 | tf_op jit(solution)/shard_map/reduce_scatter | solution.py:239
  564.2 98.6 %reduce-scatter.15.cloned.1.call-start = ((), (), s32[]{:S(2)}) async-start(), calls=%async_computation.18 | async-start | bytes 1310720 | tf_op jit(solution)/shard_map/reduce_scatter | solution.py:291
  617.7 118.8 %reduce-scatter.17.cloned.1.call-start = ((), (), s32[]{:S(2)}) async-start(), calls=%async_computation.19 | async-start | bytes 10616832 | tf_op jit(solution)/shard_map/reduce_scatter | solution.py:302
  664.4 66.1 %copy-start.68 = (s32[256]{0:T(256)S(1)}, s32[256]{0:T(256)}, u32[]{:S(2)}) copy-start(s32[256]{0:T(256)} %copy-done.67) | copy-start | bytes 3076
  677.4 53.1 %all-to-all-start.1 = ((bf16[8,32,1024]{2,1,0:T(8,128)(2,1)}), bf16[8,32,1024]{2,1,0:T(8,128)(2,1)S(1)}, u32[]{:S(2)}, u32[]{:S(2)}) async-start(bf16[8,32,1024]{2,1,0:T(8,128)(2,1)} %bitcast.46), calls=%async_computation.6 | async-start | bytes 1048576 | tf_op jit(solution)/shard_map/all_to_all | solution.py:108
  (68 other events, 544.4 us)
Sparse Core Ops, SparseCore 0:
  27.2 27.3 all-gather.9
  57.0 58.0 all-gather.11
  117.3 27.9 all-gather.15
  147.3 80.1 all-gather.21
  229.2 53.2 all-gather.17
  284.2 54.2 all-gather.13
  389.6 71.4 reduce-scatter.10
  463.4 27.2 reduce-scatter.12
  494.2 69.9 reduce-scatter.6
  565.6 27.9 all-gather.19
  595.9 26.6 reduce-scatter.8
  625.4 25.7 reduce-scatter.14
  654.7 81.7 reduce-scatter.16
